TPU v7x, 128 devices: a whole 4x4x4 slice. The times are simulated.
128 devices in a mesh: wide: 32 (over z, y, core), narrow: 4 (over x).
Axes of the slice: x: 4, y: 4, z: 4, core: 2. Of those that a mesh axis runs over, the one named last changes fastest.
Arguments:
- frames: float32 [131072, 440], P(('wide', 'narrow')), may hold values from -8 to 8
- targets: float32 [131072, 2048], P(('wide', 'narrow')), may hold values from -7 to 7
- projection: float32 [128, 440, 512], P(('wide', 'narrow')), may hold values from -0.25 to 0.25
- phases: float32 [128, 512], P(('wide', 'narrow')), may hold values from 0 to 6.283185
- block_order: int32 [128], replicated, may hold values from 0 to 127, each once
Outputs:
- residual: float32 [131072, 2048], P(('wide', 'narrow'))
- weights: float32 [2, 512, 2048], replicated
Inputs may be any that keep to these rules, and one draw needn't show every extreme that they name: `block_order`: a permutation; steps use its first 2 entries.
All inputs are finite; a program needn't handle non-finite values.
Results may differ from a plain program's by a relative error of at most 0.0003.
Values sent between devices are 32-bit elements; how exact they have to be, the bound alone decides.
A program may use at most 128 MiB of HBM per device.

v0:
```python
import jax
import jax.numpy as jnp
from jax import lax
from jax.sharding import PartitionSpec as P

STEPS = 2


def from_root(value, axis, source):
    kept = jnp.where(lax.axis_index(axis) == source, value, 0).astype(value.dtype)
    return lax.psum(kept, axis)


def features_of(frames, block_proj, block_phase):
    inner = jnp.dot(
        frames, block_proj, precision=lax.Precision.HIGHEST, preferred_element_type=jnp.float32
    )
    return jnp.sqrt(2.0 / block_proj.shape[1]) * jnp.cos(inner + block_phase[None, :])


def local_product(left, right):
    return jnp.dot(
        left.T, right, precision=lax.Precision.HIGHEST, preferred_element_type=jnp.float32
    )


def solve_block(gram_sum, cross_sum):
    width = gram_sum.shape[0]
    damping = 0.1 * jnp.trace(gram_sum) / width
    factor = jnp.linalg.cholesky(gram_sum + damping * jnp.eye(width, dtype=gram_sum.dtype))
    return jax.scipy.linalg.cho_solve((factor, True), cross_sum)


def per_device(frames, targets, projection, phases, block_order):
    feature_list = []
    for step_index in range(STEPS):
        block_proj, block_phase = (
            from_root(projection, ("wide", "narrow"), block_order[step_index]),
            from_root(phases, ("wide", "narrow"), block_order[step_index]),
        )
        feature_list.append(features_of(frames, block_proj[0], block_phase[0]))
    grams_local = jnp.stack([local_product(feats, feats) for feats in feature_list])
    grams_all = lax.psum(grams_local, ("wide", "narrow"))
    residual = targets
    solved = []
    for step_index in range(STEPS):
        feats = feature_list[step_index]
        cross_local = local_product(feats, residual)
        gram_sum = grams_all[step_index]
        cross_sum = lax.psum(cross_local, ("wide", "narrow"))
        weights = solve_block(gram_sum, cross_sum)
        residual = residual - jnp.dot(
            feats, weights, precision=lax.Precision.HIGHEST, preferred_element_type=jnp.float32
        )
        solved.append(weights)
    return (residual, jnp.stack(solved))


def solution(mesh):
    return jax.shard_map(
        per_device,
        mesh=mesh,
        in_specs=(
            P(("wide", "narrow"), None),
            P(("wide", "narrow"), None),
            P(("wide", "narrow"), None, None),
            P(("wide", "narrow"), None),
            P(),
        ),
        out_specs=(P(("wide", "narrow"), None), P()),
        check_vma=False,
    )
```

profile of v0, /device:TPU:1, one launch (start us, length us, event | category | flops | bytes accessed | tf_op | source)
XLA Modules:
  0.0 860.8 jit_solution(9181122696572727834)
XLA Ops:
  9.9 2.6 select_bitcast_fusion
  12.6 69.1 %all-reduce.1 = (f32[512]{0:T(512)S(1)}, f32[512]{0:T(512)S(1)}) all-reduce(f32[512]{0:T(512)S(1)} %bitcast.163, f32[512]{0:T(512)S(1)} %bitcast.162), channel_id=1, replica_groups=mesh['wide'=32,'narrow'=4] {'wide','narrow'}, use_global_device_ids=true, to_apply=%region_1.2 | all-reduce | flops 1024 | bytes 8192 | tf_op jit(solution)/shard_map/psum | solution.py:11
  81.7 85.6 %all-reduce.12.cloned.1.call-done = (f32[440,512]{1,0:T(8,128)}, f32[440,512]{1,0:T(8,128)}) async-done(((f32[440,512]{1,0:T(8,128)}, f32[440,512]{1,0:T(8,128)}), (f32[440,512]{1,0:T(8,128)}, f32[440,512]{1,0:T(8,128)})) %all-reduce.12.cloned.1.call-update) | async-done | bytes 1802256 | tf_op jit(solution)/shard_map/psum | solution.py:11
  167.3 11.2 %cosine_multiply_fusion.1 = f32[512,1024]{1,0:T(8,128)S(1)} fusion(f32[440,512]{1,0:T(8,128)} %get-tuple-element.42, f32[1024,440]{0,1:T(8,128)S(1)} %copy-done, f32[512]{0:T(512)S(1)} %get-tuple-element.38), kind=kOutput, calls=%fused_computation.61 | convolution fusion | flops 2769289216 | bytes 4802560 | tf_op jit(solution)/shard_map/dot_general | solution.py:15
  178.6 3.8 convolution_bitcast_fusion.1
  182.4 10.3 %cosine_multiply_fusion = f32[512,1024]{1,0:T(8,128)S(1)} fusion(f32[440,512]{1,0:T(8,128)S(1)} %copy-done.17, f32[1024,440]{0,1:T(8,128)S(1)} %copy-done, f32[512]{0:T(512)S(1)} %get-tuple-element.39), kind=kOutput, calls=%fused_computation.60 | convolution fusion | flops 2769289216 | bytes 4802560 | tf_op jit(solution)/shard_map/dot_general | solution.py:15
  194.0 3.6 convolution_bitcast_fusion
  197.7 15.2 %fusion.117 = f32[512,2048]{1,0:T(8,128)} fusion(f32[512,1024]{1,0:T(8,128)S(1)} %cosine_multiply_fusion.1, f32[1024,2048]{1,0:T(8,128)S(1)} %bitcast.159), kind=kOutput, calls=%fused_computation.198 | convolution fusion | flops 12884901888 | bytes 14680064 | tf_op jit(solution)/shard_map/dot_general | solution.py:22
  214.9 156.2 %all-reduce.10.cloned.1.call-done = (f32[512,2048]{1,0:T(8,128)}, f32[2,512,512]{1,2,0:T(8,128)}) async-done(((f32[512,2048]{1,0:T(8,128)}, f32[2,512,512]{1,2,0:T(8,128)}), (f32[512,2048]{1,0:T(8,128)}, f32[2,512,512]{1,2,0:T(8,128)})) %all-reduce.10.cloned.1.call-update) | async-done | bytes 6291472 | tf_op jit(solution)/shard_map/psum | solution.py:50
  371.1 2.3 select_reduce_fusion
  378.2 2.7 fusion.54
  381.9 11.7 %cholesky.358 = f32[128,128]{1,0:T(8,128)S(1)} custom-call(f32[128,128]{1,0:T(8,128)S(1)} %cholesky.439), custom_call_target="Cholesky" | custom-call | tf_op jit(solution)/shard_map/jit(cholesky)/cholesky | solution.py:30
  394.4 11.7 %cholesky.286 = f32[128,128]{1,0:T(8,128)S(1)} custom-call(f32[128,128]{1,0:T(8,128)S(1)} %cholesky.426), custom_call_target="Cholesky" | custom-call | tf_op jit(solution)/shard_map/jit(cholesky)/cholesky | solution.py:30
  406.9 9.8 %custom-call.29 = f32[1,128,128]{1,2,0:T(8,128)S(1)} custom-call(f32[1,128,128]{2,1,0:T(8,128)S(1)} %get-tuple-element.71), custom_call_target="InvertDiagBlocksLowerTriangular" | custom-call | tf_op jit(solution)/shard_map/jit(cholesky)/cholesky | solution.py:30
  417.4 10.0 %custom-call.33 = f32[1,128,128]{1,2,0:T(8,128)S(1)} custom-call(f32[1,128,128]{2,1,0:T(8,128)S(1)} %get-tuple-element.61), custom_call_target="InvertDiagBlocksLowerTriangular" | custom-call | tf_op jit(solution)/shard_map/jit(cholesky)/cholesky | solution.py:30
  430.0 11.7 %cholesky.377 = f32[128,128]{1,0:T(8,128)S(1)} custom-call(f32[128,128]{1,0:T(8,128)S(1)} %cholesky.443), custom_call_target="Cholesky" | custom-call | tf_op jit(solution)/shard_map/jit(cholesky)/cholesky | solution.py:30
  442.4 9.8 %custom-call.34 = f32[1,128,128]{1,2,0:T(8,128)S(1)} custom-call(f32[1,128,128]{2,1,0:T(8,128)S(1)} %get-tuple-element.58), custom_call_target="InvertDiagBlocksLowerTriangular" | custom-call | tf_op jit(solution)/shard_map/jit(cholesky)/cholesky | solution.py:30
  453.8 11.9 %cholesky.398 = f32[128,128]{1,0:T(8,128)S(1)} custom-call(f32[128,128]{1,0:T(8,128)S(1)} %cholesky.448), custom_call_target="Cholesky" | custom-call | tf_op jit(solution)/shard_map/jit(cholesky)/cholesky | solution.py:30
  465.7 9.8 %custom-call.35 = f32[1,128,128]{1,2,0:T(8,128)S(1)} custom-call(f32[1,128,128]{2,1,0:T(8,128)S(1)} %get-tuple-element.55), custom_call_target="InvertDiagBlocksLowerTriangular" | custom-call | tf_op jit(solution)/shard_map/jit(cholesky)/cholesky | solution.py:30
  477.0 11.7 %cholesky.415 = f32[128,128]{1,0:T(8,128)S(1)} custom-call(f32[128,128]{1,0:T(8,128)S(1)} %convolution_subtract_fusion.14), custom_call_target="Cholesky" | custom-call | tf_op jit(solution)/shard_map/jit(cholesky)/cholesky | solution.py:30
  489.6 11.7 %cholesky.305 = f32[128,128]{1,0:T(8,128)S(1)} custom-call(f32[128,128]{1,0:T(8,128)S(1)} %cholesky.430), custom_call_target="Cholesky" | custom-call | tf_op jit(solution)/shard_map/jit(cholesky)/cholesky | solution.py:30
  501.9 10.2 %custom-call.30 = f32[1,128,128]{1,2,0:T(8,128)S(1)} custom-call(f32[1,128,128]{2,1,0:T(8,128)S(1)} %get-tuple-element.68), custom_call_target="InvertDiagBlocksLowerTriangular" | custom-call | tf_op jit(solution)/shard_map/jit(cholesky)/cholesky | solution.py:30
  512.9 11.7 %cholesky.326 = f32[128,128]{1,0:T(8,128)S(1)} custom-call(f32[128,128]{1,0:T(8,128)S(1)} %cholesky.435), custom_call_target="Cholesky" | custom-call | tf_op jit(solution)/shard_map/jit(cholesky)/cholesky | solution.py:30
  525.3 9.8 %custom-call.31 = f32[1,128,128]{1,2,0:T(8,128)S(1)} custom-call(f32[1,128,128]{2,1,0:T(8,128)S(1)} %get-tuple-element.65), custom_call_target="InvertDiagBlocksLowerTriangular" | custom-call | tf_op jit(solution)/shard_map/jit(cholesky)/cholesky | solution.py:30
  535.7 11.9 %cholesky.343 = f32[128,128]{1,0:T(8,128)S(1)} custom-call(f32[128,128]{1,0:T(8,128)S(1)} %convolution_subtract_fusion.15), custom_call_target="Cholesky" | custom-call | tf_op jit(solution)/shard_map/jit(cholesky)/cholesky | solution.py:30
  551.0 8.3 while.4
  559.4 39.3 %custom-call.32 = f32[4,128,128]{1,2,0:T(8,128)S(1)} custom-call(f32[4,128,128]{2,1,0:T(8,128)S(1)} %get-tuple-element.18), custom_call_target="InvertDiagBlocksLowerTriangular" | custom-call | tf_op jit(solution)/shard_map/jit(_cho_solve)/triangular_solve | solution.py:31
  598.7 2.3 fusion.52
  601.0 2.4 convolution_subtract_fusion.9
  611.0 2.0 convolution_subtract_fusion.8
  614.1 2.5 convolution_subtract_fusion.4
  617.7 3.6 fusion.30
  623.3 16.1 %convolution_subtract_fusion.1 = f32[1024,2048]{1,0:T(8,128)S(1)} fusion(f32[1024,2048]{1,0:T(8,128)S(1)} %bitcast.161, f32[512,1024]{1,0:T(8,128)S(1)} %copy-done.6, f32[128,2048]{1,0:T(8,128)S(1)} %fusion.95, f32[128,2048]{1,0:T(8,128)} %copy-done.7, f32[128,2048]{1,0:T(8,128)} %copy-done.9, f32[128,2048]{1,0:T(8,128)} %fusion.90), kind=kOutput, calls=%fused_computation.8 | convolution fusion | flops 12890144768 | bytes 23068672 | tf_op jit(solution)/shard_map/dot_general | solution.py:52
  639.5 3.4 copy-done.2
  642.8 15.6 %fusion.118 = f32[512,2048]{1,0:T(8,128)} fusion(f32[512,1024]{1,0:T(8,128)S(1)} %copy-done.4, f32[1024,2048]{1,0:T(8,128)S(1)} %convolution_subtract_fusion.1), kind=kOutput, calls=%fused_computation.199 | convolution fusion | flops 12884901888 | bytes 14680064 | tf_op jit(solution)/shard_map/dot_general | solution.py:22
  662.2 2.3 select_select_fusion
  664.6 11.9 %while.5 = (s32[]{:T(128)}, f32[512,512]{1,0:T(8,128)}, s32[4,2]{0,1:T(2,128)S(1)}, f32[4,128,128]{2,1,0:T(8,128)S(1)}, s32[]{:T(128)}) while((s32[]{:T(128)}, f32[512,512]{1,0:T(8,128)}, s32[4,2]{0,1:T(2,128)S(1)}, f32[4,128,128]{2,1,0:T(8,128)S(1)}, s32[]{:T(128)}) %tuple.74), condition=%wide.while_cond.clone, body=%wide.while_body.clone.sunk | while | flops 2 | bytes 131189 | solution.py:31
  665.3 2.3 bitcast_dynamic-update-slice_fusion.5
  668.3 2.3 bitcast_dynamic-update-slice_fusion.5
  671.3 2.3 bitcast_dynamic-update-slice_fusion.5
  674.3 2.2 bitcast_dynamic-update-slice_fusion.5
  677.2 40.3 %custom-call.36 = f32[4,128,128]{1,2,0:T(8,128)S(1)} custom-call(f32[4,128,128]{2,1,0:T(8,128)} %copy-done.18), custom_call_target="InvertDiagBlocksLowerTriangular" | custom-call | tf_op jit(solution)/shard_map/jit(_cho_solve)/triangular_solve | solution.py:31
  717.5 4.2 fusion.37
  721.7 89.9 %all-reduce.8.cloned.1.call-done = f32[512,2048]{1,0:T(8,128)} async-done(((f32[512,2048]{1,0:T(8,128)}), f32[512,2048]{1,0:T(8,128)}) %all-reduce.8.cloned.1.call-update) | async-done | bytes 4194320 | tf_op jit(solution)/shard_map/psum | solution.py:50
  811.7 2.3 fusion.50
  814.0 2.5 convolution_subtract_fusion.7
  831.7 16.0 %convolution_subtract_fusion = f32[1024,2048]{1,0:T(8,128)} fusion(f32[1024,2048]{1,0:T(8,128)S(1)} %bitcast.157, f32[512,1024]{1,0:T(8,128)S(1)} %copy-done.4, f32[128,2048]{1,0:T(8,128)S(1)} %fusion.102, f32[128,2048]{1,0:T(8,128)S(1)} %fusion.100, f32[128,2048]{1,0:T(8,128)S(1)} %fusion.98, f32[128,2048]{1,0:T(8,128)S(1)} %fusion.97), kind=kOutput, calls=%fused_computation.7 | convolution fusion | flops 12890144768 | bytes 23068672 | tf_op jit(solution)/shard_map/dot_general | solution.py:52
  849.9 4.0 pad_maximum_fusion
  (149 shorter events, 64.0 us)
Async XLA Ops:
  7.2 160.2 %copy-start = (f32[1024,440]{0,1:T(8,128)S(1)}, f32[1024,440]{0,1:T(8,128)}, u32[]{:S(2)}) copy-start(f32[1024,440]{0,1:T(8,128)} %param.8) | copy-start | bytes 5406724
  7.2 5.4 copy-start.19
  7.2 160.1 %all-reduce.12.cloned.1.call-start = ((), (), s32[]{:S(2)}) async-start(), calls=%async_computation.2 | async-start | bytes 3604480 | tf_op jit(solution)/shard_map/psum | solution.py:11
  12.6 358.6 %all-reduce.10.cloned.1.call-start = ((), (), s32[]{:S(2)}) async-start(), calls=%async_computation.1 | async-start | bytes 12582912 | tf_op jit(solution)/shard_map/psum | solution.py:50
  178.6 19.1 %copy-start.5 = (f32[512,1024]{1,0:T(8,128)}, f32[512,1024]{1,0:T(8,128)S(1)}, u32[]{:S(2)}) copy-start(f32[512,1024]{1,0:T(8,128)S(1)} %cosine_multiply_fusion.1) | copy-start | bytes 6291460
  178.6 3.8 copy-start.17
  178.6 19.0 %slice-start.2 = ((s8[8388608]{0:T(1024)(128)(4,1)}), s8[4194304]{0:T(1024)(128)(4,1)S(1)}, s32[]{:S(2)}) async-start(s8[8388608]{0:T(1024)(128)(4,1)} %bitcast.158), calls=%async_computation.5 | async-start | bytes 8388608
  182.4 15.3 %slice-start.3 = ((s8[8388608]{0:T(1024)(128)(4,1)}), s8[4194304]{0:T(1024)(128)(4,1)S(1)}, s32[]{:S(2)}) async-start(s8[8388608]{0:T(1024)(128)(4,1)} %bitcast.158), calls=%async_computation.6 | async-start | bytes 8388608
  192.7 1.3 copy-start.3
  214.4 597.3 %all-reduce.8.cloned.1.call-start = ((), (), s32[]{:S(2)}) async-start(), calls=%async_computation | async-start | bytes 8388608 | tf_op jit(solution)/shard_map/psum | solution.py:50
  380.8 1.0 copy-start.16
  381.9 107.0 %copy-start.15 = (f32[512,512]{1,0:T(8,128)S(1)}, f32[512,512]{1,0:T(8,128)}, u32[]{:S(2)}) copy-start(f32[512,512]{1,0:T(8,128)} %get-tuple-element.81) | copy-start | bytes 3145732
  488.7 62.2 %copy-start.10 = (f32[512,512]{1,0:T(8,128)}, f32[512,512]{1,0:T(8,128)S(1)}, u32[]{:S(2)}) copy-start(f32[512,512]{1,0:T(8,128)S(1)} %get-tuple-element.53) | copy-start | bytes 3145732
  559.4 47.4 %copy-start.12 = (f32[512,512]{1,0:T(8,128)}, f32[512,512]{1,0:T(8,128)S(1)}, u32[]{:S(2)}) copy-start(f32[512,512]{1,0:T(8,128)S(1)} %get-tuple-element.187) | copy-start | bytes 3145732
  601.0 3.5 copy-start.13
  610.9 12.3 %slice-start.4 = ((s8[8388608]{0:T(1024)(128)(4,1)}), s8[4194304]{0:T(1024)(128)(4,1)S(1)}, s32[]{:S(2)}) async-start(s8[8388608]{0:T(1024)(128)(4,1)} %bitcast.160), calls=%async_computation.7 | async-start | bytes 8388608
  614.0 7.2 copy-start.7
  616.6 6.7 slice-start.5
  617.6 3.7 copy-start.9
  617.7 5.6 copy-start.6
  623.3 19.5 %copy-start.4 = (f32[512,1024]{1,0:T(8,128)S(1)}, f32[512,1024]{1,0:T(8,128)}, u32[]{:S(2)}) copy-start(f32[512,1024]{1,0:T(8,128)} %copy-done.3) | copy-start | bytes 6291460
  639.4 3.4 copy-start.2
  676.5 0.7 copy-start.18
  813.9 3.5 copy-start.11
  814.0 3.5 copy-start.14
  825.0 6.7 slice-start
  827.5 4.1 slice-start.1
  847.7 2.2 copy-start.8
  849.9 4.0 copy-start.1
Sparse Core Ops, SparseCore 0:
  13.6 153.6 all-reduce.11
  214.5 156.5 all-reduce.9
  658.6 153.0 all-reduce.7
where the time goes:
time: 871 us; the launch traced here: 861 us
  waiting for transfers between devices  332 us (38%)
  other arithmetic  261 us (30%)
  matrix products  143 us (16%)
  blocking collectives  69.1 us (8%)
  local copies, waits for them, and re-layouts  32.4 us (4%)
  between operations  22.6 us (3%)
    psum x2, waiting for transfers between devices, per_device(): cross_sum = lax.psum(cross_local, ('wide', 'narrow'))  246 us
    another operation x30, other arithmetic, solve_block(): jnp.linalg.cholesky(gram_sum + damping * jnp.eye(width, dtype=gram_sum.dt...  159 us
    psum x1, waiting for transfers between devices, from_root(): return lax.psum(kept, axis)  85.6 us
    another operation x5, other arithmetic, solve_block(): return jax.scipy.linalg.cho_solve((factor, True), cross_sum)  82.1 us
    psum x1, blocking collectives, from_root(): return lax.psum(kept, axis)  69.1 us
    another operation x28, matrix products, solve_block(): return jax.scipy.linalg.cho_solve((factor, True), cross_sum)  44.2 us
    dot_general x4, matrix products, local_product(): jnp.dot(left.T, right, precision=lax.Precision.HIGHEST, preferred_element...  38.1 us
    dot_general x2, matrix products, per_device(): jnp.dot(feats, weights, precision=lax.Precision.HIGHEST, preferred_elemen...  32.2 us
  transfers between devices with their start and end apart: 3, of which 3 were waited for; matrix products, arithmetic and copies ran while one was open for 7% of the time, Pallas kernels for 0%

commit v1 on v0

v1 whole, which is shorter than its diff:
```python
import jax
import jax.numpy as jnp
from jax import lax
from jax.experimental import pallas as pl
from jax.experimental.pallas import tpu as pltpu
from jax.sharding import PartitionSpec as P

STEPS = 2
FEATS = 512
MESH = pl.DeviceIdType.MESH
AXES = "xyz"
ORDERS = ("xyz", "yzx", "zxy")
HIGHEST = lax.Precision.HIGHEST
BF16 = jnp.bfloat16
F32 = jnp.float32
TN, NN, NT = ((0,), (0,)), ((1,), (0,)), ((1,), (1,))


def position():
    wide = lax.axis_index("wide")
    return {
        "x": lax.axis_index("narrow"),
        "y": lax.rem(lax.div(wide, 2), 4),
        "z": lax.div(wide, 8),
        "c": lax.rem(wide, 2),
    }


def device_of(pos):
    return ((pos["z"] * 4 + pos["y"]) * 2 + pos["c"], pos["x"])


def moved(pos, axis, step):
    new = dict(pos)
    if axis == "c":
        new["c"] = 1 - pos["c"]
    else:
        new[axis] = lax.rem(pos[axis] + step, 4)
    return new


def greet(pos):
    barrier = pltpu.get_barrier_semaphore()
    peers = [moved(pos, "c", 1)] + [moved(pos, a, d) for a in AXES for d in (1, 2, 3)]
    for peer in peers:
        pl.semaphore_signal(barrier, inc=1, device_id=device_of(peer), device_id_type=MESH)
    pl.semaphore_wait(barrier, len(peers))


def region(pos, fixed):
    return tuple(pos[a] if a in fixed else slice(None) for a in AXES)


def remote(src, dst, send, recv, peer):
    return pltpu.make_async_remote_copy(
        src_ref=src, dst_ref=dst, send_sem=send, recv_sem=recv,
        device_id=device_of(peer), device_id_type=MESH,
    )


def scatter_copies(pos, part, lanes, landing, sems, stage):
    send, recv = sems
    copies = []
    for color, order in enumerate(ORDERS):
        lo, n = lanes[color]
        for d in (1, 2, 3):
            peer = moved(pos, order[stage], d)
            src = part.at[region(peer, order[: stage + 1]) + (slice(None), pl.ds(lo, n))]
            copies.append(remote(
                src, landing[stage][color].at[d - 1],
                send.at[stage, color, d - 1], recv.at[stage, color, d - 1], peer,
            ))
    return copies


def scatter_start(*args):
    for copy in scatter_copies(*args):
        copy.start()


def scatter_finish(pos, part, lanes, landing, sems, stage):
    copies = scatter_copies(pos, part, lanes, landing, sems, stage)
    for color, order in enumerate(ORDERS):
        lo, n = lanes[color]
        for copy in copies[3 * color : 3 * color + 3]:
            copy.wait_recv()
        at = region(pos, order[: stage + 1]) + (slice(None), pl.ds(lo, n))
        came = landing[stage][color]
        part[at] = part[at] + came[0] + came[1] + came[2]


def gather_copies(pos, whole, lanes, sems, stage, own=None):
    send, recv = sems
    copies = []
    for color, order in enumerate(ORDERS):
        lo, n = lanes[color]
        at = region(pos, order[: 3 - stage]) + (slice(None), pl.ds(lo, n))
        src = whole.at[at] if own is None else own.at[:, pl.ds(lo, n)]
        for d in (1, 2, 3):
            copies.append(remote(
                src, whole.at[at],
                send.at[stage, color, d - 1], recv.at[stage, color, d - 1],
                moved(pos, order[2 - stage], d),
            ))
    return copies


def run_copies(copies):
    for copy in copies:
        copy.start()
    for copy in copies:
        copy.wait_recv()


def halves(x):
    high = x.astype(BF16)
    return high, (x - high.astype(F32)).astype(BF16)


def dot(left, right, dims=NN, precision=None):
    return lax.dot_general(
        left, right, (dims, ((), ())), precision=precision, preferred_element_type=F32
    )


def dot3(left, right, dims):
    (lh, ll), (rh, rl) = left, right
    return dot(lh, rh, dims) + dot(lh, rl, dims) + dot(ll, rh, dims)


def scaled_cosine(angle):
    turns = jnp.round(angle * 0.15915494309189535)
    half = (angle * 0.5 - turns * 3.140625) - turns * 9.67653589793e-4
    z = half * half
    poly = -2.50521083854e-8
    for coef in (2.75573192239e-6, -1.98412698413e-4, 8.33333333333e-3, -1.66666666667e-1):
        poly = poly * z + coef
    sine = half + half * (z * poly)
    return 0.0625 - 0.125 * (sine * sine)


def wide8(x):
    return jnp.broadcast_to(x, (8, 128))


def tree(terms):
    while len(terms) > 1:
        terms = [a + b for a, b in zip(terms[::2], terms[1::2])]
    return terms[0]


def eight_pivots(tiles, at):
    lane = lax.broadcasted_iota(jnp.int32, (8, 128), 1)
    row = lax.broadcasted_iota(jnp.int32, (8, 128), 0)
    top = tiles[at // 8]
    columns = [wide8(top[:, at + j : at + j + 1]) for j in range(8)]
    d = [[wide8(columns[j][i : i + 1, :]) for j in range(8)] for i in range(8)]
    for p in range(8):
        inv = 1.0 / d[p][p]
        scaled = [inv if j == p else d[p][j] * inv for j in range(8)]
        for i in range(8):
            if i != p:
                c = d[i][p]
                d[i] = [-c * inv if j == p else d[i][j] - c * scaled[j] for j in range(8)]
        d[p] = scaled
    packed = []
    for j in range(8):
        column = d[0][j]
        for i in range(1, 8):
            column = jnp.where(row == i, d[i][j], column)
        packed.append(column)
    new = tree([packed[j] * wide8(top[j : j + 1, :]) for j in range(8)])
    for j in range(8):
        new = jnp.where(lane == at + j, packed[j], new)
    rows = [wide8(new[j : j + 1, :]) for j in range(8)]
    inside = (lane >= at) & (lane < at + 8)
    out = []
    for t, tile in enumerate(tiles):
        if t == at // 8:
            out.append(new)
        else:
            change = tree([wide8(tile[:, at + j : at + j + 1]) * rows[j] for j in range(8)])
            out.append(jnp.where(inside, 0.0, tile) - change)
    return out


def inverse128(a):
    def quarter(_, a):
        tiles = [a[8 * t : 8 * t + 8] for t in range(16)]
        for k in range(4):
            tiles = eight_pivots(tiles, 8 * k)
        return pltpu.roll(jnp.concatenate(tiles[4:] + tiles[:4], axis=0), 96, 1)

    return lax.fori_loop(0, 4, quarter, a)


def invert_block_step(matrix, strip, k):
    at = pl.ds(pl.multiple_of(k * 128, 128), 128)
    block = inverse128(matrix[at, at])
    strip[...] = dot(block, matrix[at, :], NN, HIGHEST)
    strip[:, at] = block
    column = matrix[:, at]
    matrix[:, at] = jnp.zeros_like(column)
    matrix[...] = matrix[...] - dot(column, strip[...], NN, HIGHEST)
    matrix[at, :] = strip[...]


def fit_kernel(
    mask, frames, proj, phases, targets_hbm,
    solved_hbm, fh, fl,
    targets, kept, kept_came, blocks, gram, gram_came, gram_sum, matrix, other, between, between2, strip,
    cross, cross_came, own,
    b1, b2, b3, b4, b5, b6, b7, b8, b9, g1, g2, g3, g4, g5, g6, g7, g8, g9, c1, c2, c3, c4, c5, c6, c7, c8, c9,
    bs, br, bgs, bgr, gs, gr, ggs, ggr, cs, cr, cgs, cgr, pair_send, pair_recv, local,
):
    pos = position()
    core = pos["c"]
    twin = moved(pos, "c", 1)
    spot = (pos["x"], pos["y"], pos["z"])
    sent = []

    def pair(i, src, dst):
        return remote(src, dst, pair_send.at[i], pair_recv.at[i], twin)

    load = pltpu.make_async_copy(targets_hbm, targets, local.at[0])
    load.start()

    for s in range(STEPS):
        here = mask[s, 0:1, :] > 0.5
        kept[s, 0:3] = jnp.where(here, proj[0:384, :], 0.0).reshape(3, 4, 4, 8, FEATS)
        kept[s, 3, 0] = jnp.where(here, proj[384:416, :], 0.0).reshape(4, 8, FEATS)
        kept[s, 3, 1, 0:3] = jnp.where(here, proj[416:440, :], 0.0).reshape(3, 8, FEATS)
        kept[s, 3, 1, 3] = jnp.broadcast_to(jnp.where(here, phases[...], 0.0), (8, FEATS))
        kept[s, 3, 2:4] = jnp.zeros((2, 4, 8, FEATS), F32)
    greet(pos)
    thirds = ((0, 128), (128, 128), (256, 256))
    landing = ((b1, b2, b3), (b4, b5, b6), (b7, b8, b9))
    swap = pair(0, kept.at[1 - core], kept_came)
    swap.start()
    sent.append(swap)
    swap.wait_recv()
    kept[core] = kept[core] + kept_came[...]
    part = kept.at[core]
    for stage in range(3):
        scatter_start(pos, part, thirds, landing, (bs, br), stage)
        sent += scatter_copies(pos, part, thirds, landing, (bs, br), stage)
        scatter_finish(pos, part, thirds, landing, (bs, br), stage)
    blocks[(core,) + spot] = kept[(core,) + spot]
    for stage in range(3):
        copies = gather_copies(pos, blocks.at[core], thirds, (bgs, bgr), stage)
        run_copies(copies)
        sent += copies
    swap = pair(1, blocks.at[core], blocks.at[core])
    swap.start()
    sent.append(swap)
    swap.wait_recv()

    @pl.loop(0, 4)
    def _(i):
        rows = pl.ds(pl.multiple_of(i * 256, 256), 256)
        for s in range(STEPS):
            weights = blocks[s].reshape(512, FEATS)[:440]
            inner = dot(frames[rows, :], weights, NN, HIGHEST)
            high, low = halves(scaled_cosine(inner + blocks[s, 3, 1, 3, 0:1, :]))
            fh[rows, s * FEATS : (s + 1) * FEATS] = high
            fl[rows, s * FEATS : (s + 1) * FEATS] = low

    def feats(start, n):
        at = pl.ds(pl.multiple_of(start, 256), n)
        return fh[:, at], fl[:, at]

    def gram_half(c):
        @pl.loop(0, 2)
        def _(i):
            rows = pl.ds(i * 2, 2)
            square = dot3(feats(c * 512 + i * 256, 256), feats(c * 512, 512), TN)
            gram[c, rows, :, :, :, 0:512] = square.reshape(2, 4, 4, 8, 512)
            mixed = dot3(feats(512 + i * 256, 256), feats(c * 256, 256), TN)
            gram[c, rows, :, :, :, 512:768] = mixed.reshape(2, 4, 4, 8, 256)

    def cross_rows(c, lo, hi):
        @pl.loop(lo, hi)
        def _(i):
            at = pl.ds(pl.multiple_of(c * 1024 + i * 256, 256), 256)
            rows = dot3(halves(targets[:, at]), (fh[...], fl[...]), TN)
            cross[c, i] = rows.reshape(4, 4, 16, 1024)

    gram_half(1 - core)
    gram_swap = pair(2, gram.at[1 - core], gram_came)
    gram_swap.start()
    gram_half(core)
    load.wait()
    gram_swap.wait_recv()
    gram[core] = gram[core] + gram_came[...]
    part = gram.at[core]
    thirds = ((0, 256), (256, 256), (512, 256))
    landing = ((g1, g2, g3), (g4, g5, g6), (g7, g8, g9))
    args = (pos, part, thirds, landing, (gs, gr))
    scatter_start(*args, 0)
    cross_rows(1 - core, 0, 4)
    cross_swap = pair(3, cross.at[1 - core], cross_came)
    cross_swap.start()
    scatter_finish(*args, 0)
    scatter_start(*args, 1)
    cross_rows(core, 0, 2)
    scatter_finish(*args, 1)
    scatter_start(*args, 2)
    cross_rows(core, 2, 4)
    scatter_finish(*args, 2)
    for stage in range(3):
        sent += scatter_copies(*args, stage)
    gram_sum[spot] = gram[(core,) + spot]
    for stage in range(3):
        copies = gather_copies(pos, gram_sum, thirds, (ggs, ggr), stage)
        for copy in copies:
            copy.start()
        if stage == 0:
            cross_swap.wait_recv()

            @pl.loop(0, 4)
            def _(i):
                cross[core, i] = cross[core, i] + cross_came[i]

        for copy in copies:
            copy.wait_recv()
        sent += copies
    sent += [gram_swap, cross_swap]

    part = cross.at[core]
    thirds = ((0, 384), (384, 384), (768, 256))
    landing = ((c1, c2, c3), (c4, c5, c6), (c7, c8, c9))
    args = (pos, part, thirds, landing, (cs, cr))
    scatter_start(*args, 0)
    between[...] = gram_sum[:, :, :, :, 512:768].reshape(512, 256)
    mixed_swap = pair(4, between, between2)
    mixed_swap.start()
    square = gram_sum[:, :, :, :, 0:512].reshape(512, 512)
    eye = lax.broadcasted_iota(jnp.int32, square.shape, 0) == lax.broadcasted_iota(jnp.int32, square.shape, 1)
    trace = jnp.sum(jnp.where(eye, square, 0.0), keepdims=True)
    matrix[...] = jnp.where(eye, square + trace * (0.1 / FEATS), square)

    @pl.loop(0, 4)
    def _(k):
        invert_block_step(matrix, strip, k)

        @pl.when(k == 1)
        def _():
            scatter_finish(*args, 0)
            scatter_start(*args, 1)

        @pl.when(k == 2)
        def _():
            scatter_finish(*args, 1)
            scatter_start(*args, 2)

    inverse_swap = pair(5, matrix, other)
    inverse_swap.start()
    scatter_finish(*args, 2)
    for stage in range(3):
        sent += scatter_copies(*args, stage)
    sent += [mixed_swap, inverse_swap]

    mixed_swap.wait_recv()
    inverse_swap.wait_recv()
    mine = cross[(core,) + spot]
    first = core == 0
    inv0 = jnp.where(first, matrix[...], other[...])
    inv1 = jnp.where(first, other[...], matrix[...])
    low = jnp.where(first, between[...], between2[...])
    high = jnp.where(first, between2[...], between[...])
    w0 = dot(mine[:, :FEATS], inv0, NN, HIGHEST)
    seen = dot(w0[:, :256], low, NT, HIGHEST) + dot(w0[:, 256:], high, NT, HIGHEST)
    w1 = dot(mine[:, FEATS:] - seen, inv1, NN, HIGHEST)
    own[:, :FEATS] = w0
    own[:, FEATS:] = w1

    whole = solved_hbm.at[core]
    keep = pltpu.make_async_copy(own, whole.at[spot], local.at[1])
    keep.start()
    copies = gather_copies(pos, whole, thirds, (cgs, cgr), 0, own)
    run_copies(copies)
    keep.wait()
    sent += copies
    for stage in (1, 2):
        copies = gather_copies(pos, whole, thirds, (cgs, cgr), stage)
        run_copies(copies)
        sent += copies
    swap = pair(6, whole, whole)
    swap.start()
    swap.wait_recv()
    sent.append(swap)
    for copy in sent:
        copy.wait_send()


def landings(rows, widths):
    return [
        *[pltpu.VMEM((3, 4, 4, rows, n), F32) for n in widths],
        *[pltpu.VMEM((3, 4, rows, n), F32) for n in widths],
        *[pltpu.VMEM((3, rows, n), F32) for n in widths],
    ]


IN_VMEM = pl.BlockSpec(memory_space=pltpu.VMEM)
IN_HBM = pl.BlockSpec(memory_space=pl.ANY)


def fit(mask, frames, proj, phases, targets):
    return pl.pallas_call(
        fit_kernel,
        out_shape=(
            jax.ShapeDtypeStruct((2, 4, 4, 4, 16, 1024), F32),
            jax.ShapeDtypeStruct((1024, 1024), BF16),
            jax.ShapeDtypeStruct((1024, 1024), BF16),
        ),
        in_specs=[IN_VMEM, IN_VMEM, IN_VMEM, IN_VMEM, IN_HBM],
        out_specs=(IN_HBM, IN_VMEM, IN_VMEM),
        scratch_shapes=[
            pltpu.VMEM((1024, 2048), F32),
            pltpu.VMEM((2, 4, 4, 4, 8, FEATS), F32),
            pltpu.VMEM((4, 4, 4, 8, FEATS), F32),
            pltpu.VMEM((2, 4, 4, 4, 8, FEATS), F32),
            pltpu.VMEM((2, 4, 4, 4, 8, 768), F32),
            pltpu.VMEM((4, 4, 4, 8, 768), F32),
            pltpu.VMEM((4, 4, 4, 8, 768), F32),
            pltpu.VMEM((FEATS, FEATS), F32),
            pltpu.VMEM((FEATS, FEATS), F32),
            pltpu.VMEM((FEATS, 256), F32),
            pltpu.VMEM((FEATS, 256), F32),
            pltpu.VMEM((128, FEATS), F32),
            pltpu.VMEM((2, 4, 4, 4, 16, 1024), F32),
            pltpu.VMEM((4, 4, 4, 16, 1024), F32),
            pltpu.VMEM((16, 1024), F32),
            *landings(8, (128, 128, 256)),
            *landings(8, (256, 256, 256)),
            *landings(16, (384, 384, 256)),
            *[pltpu.SemaphoreType.DMA((3, 3, 3)) for _ in range(12)],
            pltpu.SemaphoreType.DMA((7,)),
            pltpu.SemaphoreType.DMA((7,)),
            pltpu.SemaphoreType.DMA((2,)),
        ],
        compiler_params=pltpu.CompilerParams(
            collective_id=1, has_side_effects=True, vmem_limit_bytes=60 << 20
        ),
    )(mask, frames, proj, phases, targets)


def residual_kernel(targets, solved, fh, fl, residual, weights):
    rows = solved[...]
    residual[...] = targets[...] - dot3((fh[...], fl[...]), halves(rows), NT)
    for s in range(STEPS):
        weights[s] = rows[:, s * FEATS : (s + 1) * FEATS].T


def residual_of(targets, solved, fh, fl):
    n = 256
    whole = pl.BlockSpec((1024, 1024), lambda i: (0, 0), pipeline_mode=pl.Buffered(1))
    return pl.pallas_call(
        residual_kernel,
        grid=(2048 // n,),
        out_shape=(
            jax.ShapeDtypeStruct((1024, 2048), F32),
            jax.ShapeDtypeStruct((STEPS, FEATS, 2048), F32),
        ),
        in_specs=[
            pl.BlockSpec((1024, n), lambda i: (0, i)),
            pl.BlockSpec((n, 1024), lambda i: (i, 0)),
            whole,
            whole,
        ],
        out_specs=(
            pl.BlockSpec((1024, n), lambda i: (0, i)),
            pl.BlockSpec((STEPS, FEATS, n), lambda i: (0, 0, i)),
        ),
        compiler_params=pltpu.CompilerParams(vmem_limit_bytes=48 << 20),
    )(targets, solved, fh, fl)


def per_device(frames, targets, projection, phases, block_order):
    me = lax.axis_index("wide") * 4 + lax.axis_index("narrow")
    mask = (block_order[:STEPS] == me).astype(F32)
    mask = jnp.broadcast_to(mask[:, None, None], (STEPS, 8, FEATS))
    solved, fh, fl = fit(mask, frames, projection[0], phases, targets)
    return residual_of(targets, solved.reshape(2048, 1024), fh, fl)


def solution(mesh):
    return jax.shard_map(
        per_device,
        mesh=mesh,
        in_specs=(
            P(("wide", "narrow"), None),
            P(("wide", "narrow"), None),
            P(("wide", "narrow"), None, None),
            P(("wide", "narrow"), None),
            P(),
        ),
        out_specs=(P(("wide", "narrow"), None), P()),
        check_vma=False,
    )
```

time: 871 us -> 201 us (0.23); the launches traced: 861 us -> 200 us
  waiting for transfers between devices: 332 us -> 0 us
  other arithmetic: 261 us -> 0.66 us
  Pallas kernels: 0 us -> 192 us
  matrix products: 143 us -> 0 us
  blocking collectives: 69.1 us -> 0 us
  local copies, waits for them, and re-layouts: 32.4 us -> 6.69 us
  between operations: 22.6 us -> 0.65 us
    psum x3 -> x0, waiting for transfers between devices: 332 us -> none  [the longest x2 246 us: per_device(): cross_sum = lax.psum(cross_local, ('wide', 'narrow'))]
    another operation x39 -> x0, other arithmetic: 251 us -> none  [the longest x30 159 us: solve_block(): jnp.linalg.cholesky(gram_sum + damping * jnp.eye(width, dtype=gram_sum.dt...]
    pallas_call x0 -> x2, Pallas kernels: none -> 192 us  [the longest x1 173 us: fit(): pl.pallas_call(fit_kernel, out_shape=(jax.ShapeDtypeStruct((2, 4, 4, 4, 1...]
    dot_general x8 -> x0, matrix products: 91.8 us -> none  [the longest x4 38.1 us: local_product(): jnp.dot(left.T, right, precision=lax.Precision.HIGHEST, preferred_element...]
    psum x1 -> x0, blocking collectives: 69.1 us -> none  [from_root(): return lax.psum(kept, axis)]
    another operation x40 -> x0, matrix products: 51.5 us -> none  [the longest x28 44.2 us: solve_block(): return jax.scipy.linalg.cho_solve((factor, True), cross_sum)]
    another operation x35 -> x0, local copies, waits for them, and re-layouts: 21.2 us -> none  [the longest x27 20.1 us: solve_block(): return jax.scipy.linalg.cho_solve((factor, True), cross_sum)]
  transfers between devices with their start and end apart: 3 -> 0, of which waited for: 3 -> 0; matrix products, arithmetic and copies ran while one was open for 7% -> 0% of each run, Pallas kernels for 0% -> 0%
where the time goes in v1:
time: 201 us; the launch traced here: 200 us
  Pallas kernels  192 us (96%)
  local copies, waits for them, and re-layouts  6.69 us (3%)
    pallas_call x1, Pallas kernels, fit(): pl.pallas_call(fit_kernel, out_shape=(jax.ShapeDtypeStruct((2, 4, 4, 4, 1...  173 us
    pallas_call x1, Pallas kernels, residual_of(): pl.pallas_call(residual_kernel, grid=(2048 // n,), out_shape=(jax.ShapeDt...  19.3 us
    unnamed x5, local copies, waits for them, and re-layouts  6 us

profile of v1, /device:TPU:1, one launch (start us, length us, event | category | flops | bytes accessed | tf_op | source)
XLA Modules:
  0.0 200.4 jit_solution(17581555190856345808)
XLA Ops:
  0.6 0.7 compare_convert_fusion
  1.3 0.7 broadcast_in_dim.2.mask
  2.0 2.8 %copy.7.frames = f32[1024,440]{1,0:T(8,128)} copy(f32[1024,440]{0,1:T(8,128)} %param.5) | data formatting | bytes 3604480 | tf_op args[0]
  4.8 173.1 %shard_map.68 = (f32[2,4,4,4,16,1024]{5,4,3,2,1,0:T(8,128)}, bf16[1024,1024]{1,0:T(8,128)(2,1)}, bf16[1024,1024]{1,0:T(8,128)(2,1)}) custom-call(f32[2,8,512]{2,1,0:T(8,128)} %broadcast_in_dim.2.mask, f32[1024,440]{1,0:T(8,128)} %copy.7.frames, f32[440,512]{1,0:T(8,128)} %bitcast.3, f32[1,512]{1,0:T(1,128)} %phases.1, f32[1024,2048]{1,0:T(8,128)} %targets.1), custom_call_target="tpu_custom_call" | custom-call | tf_op jit(solution)/shard_map/pallas_call | solution.py:409
  177.9 0.0 copy-start
  177.9 1.6 copy-done
  179.5 0.0 copy-start.1
  179.5 1.6 copy-done.1
  181.1 19.3 %shard_map.69 = (f32[1024,2048]{1,0:T(8,128)}, f32[2,512,2048]{2,1,0:T(8,128)}) custom-call(f32[1024,2048]{1,0:T(8,128)} %targets.1, f32[2048,1024]{1,0:T(8,128)} %bitcast.2, bf16[1024,1024]{1,0:T(8,128)(2,1)S(1)} %copy-done, bf16[1024,1024]{1,0:T(8,128)(2,1)S(1)} %copy-done.1), custom_call_target="tpu_custom_call" | custom-call | tf_op jit(solution)/shard_map/pallas_call | solution.py:458
Async XLA Ops:
  177.9 1.6 copy-start
  179.5 1.6 copy-start.1

commit v2 on v1

--- a/solution.py
+++ b/solution.py
@@ -44,7 +44,7 @@
     peers = [moved(pos, "c", 1)] + [moved(pos, a, d) for a in AXES for d in (1, 2, 3)]
     for peer in peers:
         pl.semaphore_signal(barrier, inc=1, device_id=device_of(peer), device_id_type=MESH)
-    pl.semaphore_wait(barrier, len(peers))
+    return lambda: pl.semaphore_wait(barrier, len(peers))
 
 
 def region(pos, fixed):
@@ -184,8 +184,9 @@
     return out
 
 
-def inverse128(a):
-    def quarter(_, a):
+def inverse128(a, beside):
+    def quarter(q, a):
+        beside(q)
         tiles = [a[8 * t : 8 * t + 8] for t in range(16)]
         for k in range(4):
             tiles = eight_pivots(tiles, 8 * k)
@@ -194,24 +195,43 @@
     return lax.fori_loop(0, 4, quarter, a)
 
 
-def invert_block_step(matrix, strip, k):
-    at = pl.ds(pl.multiple_of(k * 128, 128), 128)
-    block = inverse128(matrix[at, at])
-    strip[...] = dot(block, matrix[at, :], NN, HIGHEST)
-    strip[:, at] = block
-    column = matrix[:, at]
-    matrix[:, at] = jnp.zeros_like(column)
-    matrix[...] = matrix[...] - dot(column, strip[...], NN, HIGHEST)
-    matrix[at, :] = strip[...]
+def block_at(k):
+    return pl.ds(pl.multiple_of(k * 128, 128), 128)
+
+
+def invert(matrix, strip, column, after_step):
+    def update(q):
+        rows = block_at(q)
+        matrix[rows, :] = matrix[rows, :] - dot(column[rows, :], strip[...], NN, HIGHEST)
+
+    def step(k, diagonal):
+        at, following = block_at(k), block_at(lax.rem(k + 1, 4))
+        block = inverse128(diagonal, update)
+        strip[...] = dot(block, matrix[at, :], NN, HIGHEST)
+        strip[:, at] = block
+        column[...] = matrix[:, at]
+        column[at, :] = jnp.zeros((128, 128), F32)
+        matrix[:, at] = jnp.zeros((FEATS, 128), F32)
+        matrix[at, :] = strip[...]
+        after_step(k)
+        return matrix[following, following] - dot(
+            column[following, :], strip[:, following], NN, HIGHEST
+        )
+
+    strip[...] = jnp.zeros_like(strip)
+    column[...] = jnp.zeros_like(column)
+    lax.fori_loop(0, 4, step, matrix[block_at(0), block_at(0)])
+    for q in range(4):
+        update(q)
 
 
 def fit_kernel(
-    mask, frames, proj, phases, targets_hbm,
-    solved_hbm, fh, fl,
-    targets, kept, kept_came, blocks, gram, gram_came, gram_sum, matrix, other, between, between2, strip,
+    mask, proj, phases, frames_hbm, targets_hbm,
+    solved_hbm, fh_hbm, fl_hbm,
+    fh, fl, frames, frames_high, frames_low, proj_high, proj_low, targets, kept, kept_came, blocks, gram, gram_came, gram_sum, matrix, other, between, between2, strip, column,
     cross, cross_came, own,
     b1, b2, b3, b4, b5, b6, b7, b8, b9, g1, g2, g3, g4, g5, g6, g7, g8, g9, c1, c2, c3, c4, c5, c6, c7, c8, c9,
-    bs, br, bgs, bgr, gs, gr, ggs, ggr, cs, cr, cgs, cgr, pair_send, pair_recv, local,
+    bs, br, bgs, bgr, gs, gr, ggs, ggr, cs, cr, cgs, cgr, pair_send, pair_recv, fwd_send, fwd_recv, local,
 ):
     pos = position()
     core = pos["c"]
@@ -222,6 +242,9 @@
     def pair(i, src, dst):
         return remote(src, dst, pair_send.at[i], pair_recv.at[i], twin)
 
+    met = greet(pos)
+    load_frames = pltpu.make_async_copy(frames_hbm, frames, local.at[2])
+    load_frames.start()
     load = pltpu.make_async_copy(targets_hbm, targets, local.at[0])
     load.start()
 
@@ -232,12 +255,21 @@
         kept[s, 3, 1, 0:3] = jnp.where(here, proj[416:440, :], 0.0).reshape(3, 8, FEATS)
         kept[s, 3, 1, 3] = jnp.broadcast_to(jnp.where(here, phases[...], 0.0), (8, FEATS))
         kept[s, 3, 2:4] = jnp.zeros((2, 4, 8, FEATS), F32)
-    greet(pos)
+    met()
     thirds = ((0, 128), (128, 128), (256, 256))
     landing = ((b1, b2, b3), (b4, b5, b6), (b7, b8, b9))
     swap = pair(0, kept.at[1 - core], kept_came)
     swap.start()
     sent.append(swap)
+    load_frames.wait()
+
+    @pl.loop(0, 4)
+    def _(i):
+        at = pl.ds(pl.multiple_of(i * 256, 256), 256)
+        high, low = halves(frames[:, at])
+        frames_high[:, at] = high
+        frames_low[:, at] = low
+
     swap.wait_recv()
     kept[core] = kept[core] + kept_came[...]
     part = kept.at[core]
@@ -253,17 +285,32 @@
     swap = pair(1, blocks.at[core], blocks.at[core])
     swap.start()
     sent.append(swap)
+
+    def features(s):
+        high, low = halves(blocks[s].reshape(512, FEATS)[:440])
+        proj_high[...] = high
+        proj_low[...] = low
+        lanes = pl.ds(pl.multiple_of(s * FEATS, FEATS), FEATS)
+
+        @pl.loop(0, 4)
+        def _(i):
+            rows = pl.ds(pl.multiple_of(i * 256, 256), 256)
+            inner = dot3(
+                (frames_high[:, rows], frames_low[:, rows]), (proj_high[...], proj_low[...]), TN
+            )
+            high, low = halves(scaled_cosine(inner + blocks[s, 3, 1, 3, 0:1, :]))
+            fh[rows, lanes] = high
+            fl[rows, lanes] = low
+
+    features(core)
     swap.wait_recv()
-
-    @pl.loop(0, 4)
-    def _(i):
-        rows = pl.ds(pl.multiple_of(i * 256, 256), 256)
-        for s in range(STEPS):
-            weights = blocks[s].reshape(512, FEATS)[:440]
-            inner = dot(frames[rows, :], weights, NN, HIGHEST)
-            high, low = halves(scaled_cosine(inner + blocks[s, 3, 1, 3, 0:1, :]))
-            fh[rows, s * FEATS : (s + 1) * FEATS] = high
-            fl[rows, s * FEATS : (s + 1) * FEATS] = low
+    features(1 - core)
+    stores = [
+        pltpu.make_async_copy(fh, fh_hbm, local.at[3]),
+        pltpu.make_async_copy(fl, fl_hbm, local.at[4]),
+    ]
+    for store in stores:
+        store.start()
 
     def feats(start, n):
         at = pl.ds(pl.multiple_of(start, 256), n)
@@ -339,10 +386,7 @@
     trace = jnp.sum(jnp.where(eye, square, 0.0), keepdims=True)
     matrix[...] = jnp.where(eye, square + trace * (0.1 / FEATS), square)
 
-    @pl.loop(0, 4)
-    def _(k):
-        invert_block_step(matrix, strip, k)
-
+    def after_step(k):
         @pl.when(k == 1)
         def _():
             scatter_finish(*args, 0)
@@ -352,6 +396,8 @@
         def _():
             scatter_finish(*args, 1)
             scatter_start(*args, 2)
+
+    invert(matrix, strip, column, after_step)
 
     inverse_swap = pair(5, matrix, other)
     inverse_swap.start()
@@ -381,14 +427,31 @@
     run_copies(copies)
     keep.wait()
     sent += copies
-    for stage in (1, 2):
-        copies = gather_copies(pos, whole, thirds, (cgs, cgr), stage)
-        run_copies(copies)
-        sent += copies
-    swap = pair(6, whole, whole)
-    swap.start()
-    swap.wait_recv()
-    sent.append(swap)
+    copies = gather_copies(pos, whole, thirds, (cgs, cgr), 1)
+    run_copies(copies)
+    sent += copies
+    copies = gather_copies(pos, whole, thirds, (cgs, cgr), 2)
+    for copy in copies:
+        copy.start()
+    sent += copies
+
+    forwarded = []
+    for d in (0, 1, 3, 2):
+        for color, order in enumerate(ORDERS):
+            lo, n = thirds[color]
+            origin = pos
+            if d:
+                copies[3 * color + d - 1].wait_recv()
+                origin = moved(pos, order[0], 4 - d)
+            at = region(origin, order[:1]) + (slice(None), pl.ds(lo, n))
+            copy = remote(whole.at[at], whole.at[at], fwd_send.at[color, d], fwd_recv.at[color, d], twin)
+            copy.start()
+            forwarded.append(copy)
+    for copy in forwarded:
+        copy.wait_recv()
+    sent += forwarded
+    for store in stores:
+        store.wait()
     for copy in sent:
         copy.wait_send()
 
@@ -405,7 +468,7 @@
 IN_HBM = pl.BlockSpec(memory_space=pl.ANY)
 
 
-def fit(mask, frames, proj, phases, targets):
+def fit(mask, proj, phases, frames, targets):
     return pl.pallas_call(
         fit_kernel,
         out_shape=(
@@ -413,9 +476,16 @@
             jax.ShapeDtypeStruct((1024, 1024), BF16),
             jax.ShapeDtypeStruct((1024, 1024), BF16),
         ),
-        in_specs=[IN_VMEM, IN_VMEM, IN_VMEM, IN_VMEM, IN_HBM],
-        out_specs=(IN_HBM, IN_VMEM, IN_VMEM),
+        in_specs=[IN_VMEM, IN_VMEM, IN_VMEM, IN_HBM, IN_HBM],
+        out_specs=(IN_HBM, IN_HBM, IN_HBM),
         scratch_shapes=[
+            pltpu.VMEM((1024, 1024), BF16),
+            pltpu.VMEM((1024, 1024), BF16),
+            pltpu.VMEM((440, 1024), F32),
+            pltpu.VMEM((440, 1024), BF16),
+            pltpu.VMEM((440, 1024), BF16),
+            pltpu.VMEM((440, FEATS), BF16),
+            pltpu.VMEM((440, FEATS), BF16),
             pltpu.VMEM((1024, 2048), F32),
             pltpu.VMEM((2, 4, 4, 4, 8, FEATS), F32),
             pltpu.VMEM((4, 4, 4, 8, FEATS), F32),
@@ -428,6 +498,7 @@
             pltpu.VMEM((FEATS, 256), F32),
             pltpu.VMEM((FEATS, 256), F32),
             pltpu.VMEM((128, FEATS), F32),
+            pltpu.VMEM((FEATS, 128), F32),
             pltpu.VMEM((2, 4, 4, 4, 16, 1024), F32),
             pltpu.VMEM((4, 4, 4, 16, 1024), F32),
             pltpu.VMEM((16, 1024), F32),
@@ -435,14 +506,16 @@
             *landings(8, (256, 256, 256)),
             *landings(16, (384, 384, 256)),
             *[pltpu.SemaphoreType.DMA((3, 3, 3)) for _ in range(12)],
-            pltpu.SemaphoreType.DMA((7,)),
-            pltpu.SemaphoreType.DMA((7,)),
-            pltpu.SemaphoreType.DMA((2,)),
+            pltpu.SemaphoreType.DMA((6,)),
+            pltpu.SemaphoreType.DMA((6,)),
+            pltpu.SemaphoreType.DMA((3, 4)),
+            pltpu.SemaphoreType.DMA((3, 4)),
+            pltpu.SemaphoreType.DMA((5,)),
         ],
         compiler_params=pltpu.CompilerParams(
             collective_id=1, has_side_effects=True, vmem_limit_bytes=60 << 20
         ),
-    )(mask, frames, proj, phases, targets)
+    )(mask, proj, phases, frames, targets)
 
 
 def residual_kernel(targets, solved, fh, fl, residual, weights):
@@ -454,7 +527,6 @@
 
 def residual_of(targets, solved, fh, fl):
     n = 256
-    whole = pl.BlockSpec((1024, 1024), lambda i: (0, 0), pipeline_mode=pl.Buffered(1))
     return pl.pallas_call(
         residual_kernel,
         grid=(2048 // n,),
@@ -465,14 +537,14 @@
         in_specs=[
             pl.BlockSpec((1024, n), lambda i: (0, i)),
             pl.BlockSpec((n, 1024), lambda i: (i, 0)),
-            whole,
-            whole,
+            IN_VMEM,
+            IN_VMEM,
         ],
         out_specs=(
             pl.BlockSpec((1024, n), lambda i: (0, i)),
             pl.BlockSpec((STEPS, FEATS, n), lambda i: (0, 0, i)),
         ),
-        compiler_params=pltpu.CompilerParams(vmem_limit_bytes=48 << 20),
+        compiler_params=pltpu.CompilerParams(vmem_limit_bytes=60 << 20),
     )(targets, solved, fh, fl)
 
 
@@ -480,7 +552,7 @@
     me = lax.axis_index("wide") * 4 + lax.axis_index("narrow")
     mask = (block_order[:STEPS] == me).astype(F32)
     mask = jnp.broadcast_to(mask[:, None, None], (STEPS, 8, FEATS))
-    solved, fh, fl = fit(mask, frames, projection[0], phases, targets)
+    solved, fh, fl = fit(mask, projection[0], phases, frames.T, targets)
     return residual_of(targets, solved.reshape(2048, 1024), fh, fl)
 
 

time: 201 us -> 188 us (0.935)
  Pallas kernels: 192 us -> 186 us
  local copies, waits for them, and re-layouts: 6.69 us -> 0.69 us
    pallas_call x1, Pallas kernels: 173 us -> 165 us  [fit(): pl.pallas_call(fit_kernel, out_shape=(jax.ShapeDtypeStruct((2, 4, 4, 4, 1...]
    unnamed x5 -> x0, local copies, waits for them, and re-layouts: 6 us -> none
where the time goes in v2:
time: 188 us
  Pallas kernels  186 us (99%)
    pallas_call x1, Pallas kernels, fit(): pl.pallas_call(fit_kernel, out_shape=(jax.ShapeDtypeStruct((2, 4, 4, 4, 1...  165 us
    pallas_call x1, Pallas kernels, residual_of(): pl.pallas_call(residual_kernel, grid=(2048 // n,), out_shape=(jax.ShapeDt...  20.7 us

profile of v2, /device:TPU:1, one launch (start us, length us, event | category | flops | bytes accessed | tf_op | source)
XLA Modules:
  0.0 187.8 jit_solution(10984558546744399119)
XLA Ops:
  0.6 0.7 compare_convert_fusion
  1.3 0.7 broadcast_in_dim.2.mask
  2.0 165.1 %shard_map.68 = (f32[2,4,4,4,16,1024]{5,4,3,2,1,0:T(8,128)}, bf16[1024,1024]{1,0:T(8,128)(2,1)}, bf16[1024,1024]{1,0:T(8,128)(2,1)}) custom-call(f32[2,8,512]{2,1,0:T(8,128)} %broadcast_in_dim.2.mask, f32[440,512]{1,0:T(8,128)} %bitcast.5, f32[1,512]{1,0:T(1,128)} %phases.1, f32[440,1024]{1,0:T(8,128)} %bitcast.4, f32[1024,2048]{1,0:T(8,128)} %targets.1), custom_call_target="tpu_custom_call" | custom-call | tf_op jit(solution)/shard_map/pallas_call | solution.py:472
  167.1 20.7 %shard_map.69 = (f32[1024,2048]{1,0:T(8,128)}, f32[2,512,2048]{2,1,0:T(8,128)}) custom-call(f32[1024,2048]{1,0:T(8,128)} %targets.1, f32[2048,1024]{1,0:T(8,128)} %bitcast.3, bf16[1024,1024]{1,0:T(8,128)(2,1)} %get-tuple-element.6.fh, bf16[1024,1024]{1,0:T(8,128)(2,1)} %get-tuple-element.7.fl), custom_call_target="tpu_custom_call" | custom-call | tf_op jit(solution)/shard_map/pallas_call | solution.py:530

commit v3 on v2

--- a/solution.py
+++ b/solution.py
@@ -199,7 +199,7 @@
     return pl.ds(pl.multiple_of(k * 128, 128), 128)
 
 
-def invert(matrix, strip, column, after_step):
+def invert(matrix, strip, column, after_step, after_band):
     def update(q):
         rows = block_at(q)
         matrix[rows, :] = matrix[rows, :] - dot(column[rows, :], strip[...], NN, HIGHEST)
@@ -223,12 +223,13 @@
     lax.fori_loop(0, 4, step, matrix[block_at(0), block_at(0)])
     for q in range(4):
         update(q)
+        after_band(q)
 
 
 def fit_kernel(
     mask, proj, phases, frames_hbm, targets_hbm,
     solved_hbm, fh_hbm, fl_hbm,
-    fh, fl, frames, frames_high, frames_low, proj_high, proj_low, targets, kept, kept_came, blocks, gram, gram_came, gram_sum, matrix, other, between, between2, strip, column,
+    fh, fl, frames, frames_high, frames_low, proj_high, proj_low, targets, kept, kept_came, blocks, gram, gram_came, gram_sum, damped, inverses, mixed, strip, column,
     cross, cross_came, own,
     b1, b2, b3, b4, b5, b6, b7, b8, b9, g1, g2, g3, g4, g5, g6, g7, g8, g9, c1, c2, c3, c4, c5, c6, c7, c8, c9,
     bs, br, bgs, bgr, gs, gr, ggs, ggr, cs, cr, cgs, cgr, pair_send, pair_recv, fwd_send, fwd_recv, local,
@@ -292,9 +293,8 @@
         proj_low[...] = low
         lanes = pl.ds(pl.multiple_of(s * FEATS, FEATS), FEATS)
 
-        @pl.loop(0, 4)
-        def _(i):
-            rows = pl.ds(pl.multiple_of(i * 256, 256), 256)
+        for i in range(4):
+            rows = slice(i * 256, i * 256 + 256)
             inner = dot3(
                 (frames_high[:, rows], frames_low[:, rows]), (proj_high[...], proj_low[...]), TN
             )
@@ -378,13 +378,18 @@
     landing = ((c1, c2, c3), (c4, c5, c6), (c7, c8, c9))
     args = (pos, part, thirds, landing, (cs, cr))
     scatter_start(*args, 0)
-    between[...] = gram_sum[:, :, :, :, 512:768].reshape(512, 256)
-    mixed_swap = pair(4, between, between2)
+    mixed[core] = gram_sum[:, :, :, :, 512:768].reshape(512, 256)
+    mixed_swap = pair(4, mixed.at[core], mixed.at[core])
     mixed_swap.start()
     square = gram_sum[:, :, :, :, 0:512].reshape(512, 512)
     eye = lax.broadcasted_iota(jnp.int32, square.shape, 0) == lax.broadcasted_iota(jnp.int32, square.shape, 1)
     trace = jnp.sum(jnp.where(eye, square, 0.0), keepdims=True)
-    matrix[...] = jnp.where(eye, square + trace * (0.1 / FEATS), square)
+    square = jnp.where(eye, square + trace * (0.1 / FEATS), square)
+    damped[core] = square
+    damped_swap = pair(5, damped.at[core], damped.at[core])
+    damped_swap.start()
+    matrix = inverses.at[core]
+    matrix[...] = square
 
     def after_step(k):
         @pl.when(k == 1)
@@ -397,26 +402,35 @@
             scatter_finish(*args, 1)
             scatter_start(*args, 2)
 
-    invert(matrix, strip, column, after_step)
-
-    inverse_swap = pair(5, matrix, other)
-    inverse_swap.start()
+    swaps = []
+
+    def after_band(q):
+        band = matrix.at[pl.ds(q * 128, 128)]
+        swap = remote(band, band, fwd_send.at[3, q], fwd_recv.at[3, q], twin)
+        swap.start()
+        swaps.append(swap)
+
+    invert(matrix, strip, column, after_step, after_band)
+
     scatter_finish(*args, 2)
     for stage in range(3):
         sent += scatter_copies(*args, stage)
-    sent += [mixed_swap, inverse_swap]
+    sent += [mixed_swap, damped_swap] + swaps
 
     mixed_swap.wait_recv()
-    inverse_swap.wait_recv()
+    damped_swap.wait_recv()
+    for swap in swaps:
+        swap.wait_recv()
     mine = cross[(core,) + spot]
-    first = core == 0
-    inv0 = jnp.where(first, matrix[...], other[...])
-    inv1 = jnp.where(first, other[...], matrix[...])
-    low = jnp.where(first, between[...], between2[...])
-    high = jnp.where(first, between2[...], between[...])
-    w0 = dot(mine[:, :FEATS], inv0, NN, HIGHEST)
-    seen = dot(w0[:, :256], low, NT, HIGHEST) + dot(w0[:, 256:], high, NT, HIGHEST)
-    w1 = dot(mine[:, FEATS:] - seen, inv1, NN, HIGHEST)
+
+    def solve(step, right):
+        guess = dot(right, inverses[step], NN, HIGHEST)
+        left_over = right - dot(guess, damped[step], NN, HIGHEST)
+        return guess + dot3(halves(left_over), halves(inverses[step]), NN)
+
+    w0 = solve(0, mine[:, :FEATS])
+    seen = dot(w0[:, :256], mixed[0], NT, HIGHEST) + dot(w0[:, 256:], mixed[1], NT, HIGHEST)
+    w1 = solve(1, mine[:, FEATS:] - seen)
     own[:, :FEATS] = w0
     own[:, FEATS:] = w1
 
@@ -493,10 +507,9 @@
             pltpu.VMEM((2, 4, 4, 4, 8, 768), F32),
             pltpu.VMEM((4, 4, 4, 8, 768), F32),
             pltpu.VMEM((4, 4, 4, 8, 768), F32),
-            pltpu.VMEM((FEATS, FEATS), F32),
-            pltpu.VMEM((FEATS, FEATS), F32),
-            pltpu.VMEM((FEATS, 256), F32),
-            pltpu.VMEM((FEATS, 256), F32),
+            pltpu.VMEM((STEPS, FEATS, FEATS), F32),
+            pltpu.VMEM((STEPS, FEATS, FEATS), F32),
+            pltpu.VMEM((2, FEATS, 256), F32),
             pltpu.VMEM((128, FEATS), F32),
             pltpu.VMEM((FEATS, 128), F32),
             pltpu.VMEM((2, 4, 4, 4, 16, 1024), F32),
@@ -508,8 +521,8 @@
             *[pltpu.SemaphoreType.DMA((3, 3, 3)) for _ in range(12)],
             pltpu.SemaphoreType.DMA((6,)),
             pltpu.SemaphoreType.DMA((6,)),
-            pltpu.SemaphoreType.DMA((3, 4)),
-            pltpu.SemaphoreType.DMA((3, 4)),
+            pltpu.SemaphoreType.DMA((4, 4)),
+            pltpu.SemaphoreType.DMA((4, 4)),
             pltpu.SemaphoreType.DMA((5,)),
         ],
         compiler_params=pltpu.CompilerParams(

time: 188 us -> 190 us (1.011)
  no operation moved by 1% of the time
where the time goes in v3:
time: 190 us; the launch traced here: 189 us
  Pallas kernels  187 us (98%)
    pallas_call x1, Pallas kernels, fit(): pl.pallas_call(fit_kernel, out_shape=(jax.ShapeDtypeStruct((2, 4, 4, 4, 1...  167 us
    pallas_call x1, Pallas kernels, residual_of(): pl.pallas_call(residual_kernel, grid=(2048 // n,), out_shape=(jax.ShapeDt...  20.7 us

profile of v3, /device:TPU:1, one launch (start us, length us, event | category | flops | bytes accessed | tf_op | source)
XLA Modules:
  0.0 189.2 jit_solution(10179826303489285702)
XLA Ops:
  0.6 0.7 compare_convert_fusion
  1.3 0.7 broadcast_in_dim.2.mask
  2.0 166.6 %shard_map.68 = (f32[2,4,4,4,16,1024]{5,4,3,2,1,0:T(8,128)}, bf16[1024,1024]{1,0:T(8,128)(2,1)}, bf16[1024,1024]{1,0:T(8,128)(2,1)}) custom-call(f32[2,8,512]{2,1,0:T(8,128)} %broadcast_in_dim.2.mask, f32[440,512]{1,0:T(8,128)} %bitcast.5, f32[1,512]{1,0:T(1,128)} %phases.1, f32[440,1024]{1,0:T(8,128)} %bitcast.4, f32[1024,2048]{1,0:T(8,128)} %targets.1), custom_call_target="tpu_custom_call" | custom-call | tf_op jit(solution)/shard_map/pallas_call | solution.py:486
  168.5 20.7 %shard_map.69 = (f32[1024,2048]{1,0:T(8,128)}, f32[2,512,2048]{2,1,0:T(8,128)}) custom-call(f32[1024,2048]{1,0:T(8,128)} %targets.1, f32[2048,1024]{1,0:T(8,128)} %bitcast.3, bf16[1024,1024]{1,0:T(8,128)(2,1)} %get-tuple-element.6.fh, bf16[1024,1024]{1,0:T(8,128)(2,1)} %get-tuple-element.7.fl), custom_call_target="tpu_custom_call" | custom-call | tf_op jit(solution)/shard_map/pallas_call | solution.py:543

commit v4 on v3

--- a/solution.py
+++ b/solution.py
@@ -232,7 +232,7 @@
     fh, fl, frames, frames_high, frames_low, proj_high, proj_low, targets, kept, kept_came, blocks, gram, gram_came, gram_sum, damped, inverses, mixed, strip, column,
     cross, cross_came, own,
     b1, b2, b3, b4, b5, b6, b7, b8, b9, g1, g2, g3, g4, g5, g6, g7, g8, g9, c1, c2, c3, c4, c5, c6, c7, c8, c9,
-    bs, br, bgs, bgr, gs, gr, ggs, ggr, cs, cr, cgs, cgr, pair_send, pair_recv, fwd_send, fwd_recv, local,
+    bs, br, bgs, bgr, gs, gr, ggs, ggr, cs, cr, cgs, cgr, pair_send, pair_recv, fwd_send, fwd_recv, deep_send, deep_recv, local,
 ):
     pos = position()
     core = pos["c"]
@@ -424,9 +424,10 @@
     mine = cross[(core,) + spot]
 
     def solve(step, right):
-        guess = dot(right, inverses[step], NN, HIGHEST)
+        inverse = halves(inverses[step])
+        guess = dot3(halves(right), inverse, NN)
         left_over = right - dot(guess, damped[step], NN, HIGHEST)
-        return guess + dot3(halves(left_over), halves(inverses[step]), NN)
+        return guess + dot3(halves(left_over), inverse, NN)
 
     w0 = solve(0, mine[:, :FEATS])
     seen = dot(w0[:, :256], mixed[0], NT, HIGHEST) + dot(w0[:, 256:], mixed[1], NT, HIGHEST)
@@ -442,23 +443,40 @@
     keep.wait()
     sent += copies
     copies = gather_copies(pos, whole, thirds, (cgs, cgr), 1)
-    run_copies(copies)
-    sent += copies
-    copies = gather_copies(pos, whole, thirds, (cgs, cgr), 2)
     for copy in copies:
         copy.start()
     sent += copies
 
-    forwarded = []
+    deep = {}
     for d in (0, 1, 3, 2):
         for color, order in enumerate(ORDERS):
             lo, n = thirds[color]
             origin = pos
             if d:
                 copies[3 * color + d - 1].wait_recv()
-                origin = moved(pos, order[0], 4 - d)
+                origin = moved(pos, order[1], 4 - d)
+            at = region(origin, order[:2]) + (slice(None), pl.ds(lo, n))
+            for e in (1, 2, 3):
+                copy = remote(
+                    whole.at[at], whole.at[at],
+                    deep_send.at[color, d, e - 1], deep_recv.at[color, d, e - 1],
+                    moved(pos, order[0], e),
+                )
+                copy.start()
+                deep[color, d, e] = copy
+                sent.append(copy)
+
+    forwarded = []
+    for e in (0, 1, 3, 2):
+        for color, order in enumerate(ORDERS):
+            lo, n = thirds[color]
+            origin = pos
+            if e:
+                for d in range(4):
+                    deep[color, d, e].wait_recv()
+                origin = moved(pos, order[0], 4 - e)
             at = region(origin, order[:1]) + (slice(None), pl.ds(lo, n))
-            copy = remote(whole.at[at], whole.at[at], fwd_send.at[color, d], fwd_recv.at[color, d], twin)
+            copy = remote(whole.at[at], whole.at[at], fwd_send.at[color, e], fwd_recv.at[color, e], twin)
             copy.start()
             forwarded.append(copy)
     for copy in forwarded:
@@ -523,6 +541,8 @@
             pltpu.SemaphoreType.DMA((6,)),
             pltpu.SemaphoreType.DMA((4, 4)),
             pltpu.SemaphoreType.DMA((4, 4)),
+            pltpu.SemaphoreType.DMA((3, 4, 3)),
+            pltpu.SemaphoreType.DMA((3, 4, 3)),
             pltpu.SemaphoreType.DMA((5,)),
         ],
         compiler_params=pltpu.CompilerParams(

time: 190 us -> 184 us (0.968)
  Pallas kernels: 187 us -> 182 us
    pallas_call x1, Pallas kernels: 167 us -> 161 us  [fit(): pl.pallas_call(fit_kernel, out_shape=(jax.ShapeDtypeStruct((2, 4, 4, 4, 1...]
where the time goes in v4:
time: 184 us
  Pallas kernels  182 us (99%)
    pallas_call x1, Pallas kernels, fit(): pl.pallas_call(fit_kernel, out_shape=(jax.ShapeDtypeStruct((2, 4, 4, 4, 1...  161 us
    pallas_call x1, Pallas kernels, residual_of(): pl.pallas_call(residual_kernel, grid=(2048 // n,), out_shape=(jax.ShapeDt...  20.7 us

profile of v4, /device:TPU:1, one launch (start us, length us, event | category | flops | bytes accessed | tf_op | source)
XLA Modules:
  0.0 183.7 jit_solution(13156404740892855273)
XLA Ops:
  0.6 0.7 compare_convert_fusion
  1.3 0.7 broadcast_in_dim.2.mask
  2.0 161.0 %shard_map.68 = (f32[2,4,4,4,16,1024]{5,4,3,2,1,0:T(8,128)}, bf16[1024,1024]{1,0:T(8,128)(2,1)}, bf16[1024,1024]{1,0:T(8,128)(2,1)}) custom-call(f32[2,8,512]{2,1,0:T(8,128)} %broadcast_in_dim.2.mask, f32[440,512]{1,0:T(8,128)} %bitcast.5, f32[1,512]{1,0:T(1,128)} %phases.1, f32[440,1024]{1,0:T(8,128)} %bitcast.4, f32[1024,2048]{1,0:T(8,128)} %targets.1), custom_call_target="tpu_custom_call" | custom-call | tf_op jit(solution)/shard_map/pallas_call | solution.py:504
  163.0 20.7 %shard_map.69 = (f32[1024,2048]{1,0:T(8,128)}, f32[2,512,2048]{2,1,0:T(8,128)}) custom-call(f32[1024,2048]{1,0:T(8,128)} %targets.1, f32[2048,1024]{1,0:T(8,128)} %bitcast.3, bf16[1024,1024]{1,0:T(8,128)(2,1)} %get-tuple-element.6.fh, bf16[1024,1024]{1,0:T(8,128)(2,1)} %get-tuple-element.7.fl), custom_call_target="tpu_custom_call" | custom-call | tf_op jit(solution)/shard_map/pallas_call | solution.py:563

commit v5 on v4

--- a/solution.py
+++ b/solution.py
@@ -227,9 +227,9 @@
 
 
 def fit_kernel(
-    mask, proj, phases, frames_hbm, targets_hbm,
+    visited, phases, proj_hbm, frames_hbm, targets_hbm,
     solved_hbm, fh_hbm, fl_hbm,
-    fh, fl, frames, frames_high, frames_low, proj_high, proj_low, targets, kept, kept_came, blocks, gram, gram_came, gram_sum, damped, inverses, mixed, strip, column,
+    fh, fl, proj, frames, frames_high, frames_low, proj_high, proj_low, targets, kept, kept_came, blocks, gram, gram_came, gram_sum, damped, inverses, mixed, strip, column,
     cross, cross_came, own,
     b1, b2, b3, b4, b5, b6, b7, b8, b9, g1, g2, g3, g4, g5, g6, g7, g8, g9, c1, c2, c3, c4, c5, c6, c7, c8, c9,
     bs, br, bgs, bgr, gs, gr, ggs, ggr, cs, cr, cgs, cgr, pair_send, pair_recv, fwd_send, fwd_recv, deep_send, deep_recv, local,
@@ -244,13 +244,17 @@
         return remote(src, dst, pair_send.at[i], pair_recv.at[i], twin)
 
     met = greet(pos)
+    load_proj = pltpu.make_async_copy(proj_hbm, proj, local.at[5])
+    load_proj.start()
     load_frames = pltpu.make_async_copy(frames_hbm, frames, local.at[2])
     load_frames.start()
     load = pltpu.make_async_copy(targets_hbm, targets, local.at[0])
     load.start()
 
+    me = lax.axis_index("wide") * 4 + lax.axis_index("narrow")
+    load_proj.wait()
     for s in range(STEPS):
-        here = mask[s, 0:1, :] > 0.5
+        here = jnp.full((1, FEATS), visited[s], jnp.int32) == me
         kept[s, 0:3] = jnp.where(here, proj[0:384, :], 0.0).reshape(3, 4, 4, 8, FEATS)
         kept[s, 3, 0] = jnp.where(here, proj[384:416, :], 0.0).reshape(4, 8, FEATS)
         kept[s, 3, 1, 0:3] = jnp.where(here, proj[416:440, :], 0.0).reshape(3, 8, FEATS)
@@ -500,7 +504,7 @@
 IN_HBM = pl.BlockSpec(memory_space=pl.ANY)
 
 
-def fit(mask, proj, phases, frames, targets):
+def fit(visited, phases, proj, frames, targets):
     return pl.pallas_call(
         fit_kernel,
         out_shape=(
@@ -508,11 +512,12 @@
             jax.ShapeDtypeStruct((1024, 1024), BF16),
             jax.ShapeDtypeStruct((1024, 1024), BF16),
         ),
-        in_specs=[IN_VMEM, IN_VMEM, IN_VMEM, IN_HBM, IN_HBM],
+        in_specs=[pl.BlockSpec(memory_space=pltpu.SMEM), IN_VMEM, IN_HBM, IN_HBM, IN_HBM],
         out_specs=(IN_HBM, IN_HBM, IN_HBM),
         scratch_shapes=[
             pltpu.VMEM((1024, 1024), BF16),
             pltpu.VMEM((1024, 1024), BF16),
+            pltpu.VMEM((440, FEATS), F32),
             pltpu.VMEM((440, 1024), F32),
             pltpu.VMEM((440, 1024), BF16),
             pltpu.VMEM((440, 1024), BF16),
@@ -543,23 +548,24 @@
             pltpu.SemaphoreType.DMA((4, 4)),
             pltpu.SemaphoreType.DMA((3, 4, 3)),
             pltpu.SemaphoreType.DMA((3, 4, 3)),
-            pltpu.SemaphoreType.DMA((5,)),
+            pltpu.SemaphoreType.DMA((6,)),
         ],
         compiler_params=pltpu.CompilerParams(
             collective_id=1, has_side_effects=True, vmem_limit_bytes=60 << 20
         ),
-    )(mask, proj, phases, frames, targets)
+    )(visited, phases, proj, frames, targets)
 
 
 def residual_kernel(targets, solved, fh, fl, residual, weights):
-    rows = solved[...]
-    residual[...] = targets[...] - dot3((fh[...], fl[...]), halves(rows), NT)
+    columns = [solved[:, s * FEATS : (s + 1) * FEATS].T for s in range(STEPS)]
+    fitted = dot3((fh[...], fl[...]), halves(jnp.concatenate(columns, axis=0)), NN)
+    residual[...] = targets[...] - fitted
     for s in range(STEPS):
-        weights[s] = rows[:, s * FEATS : (s + 1) * FEATS].T
+        weights[s] = columns[s]
 
 
 def residual_of(targets, solved, fh, fl):
-    n = 256
+    n = 512
     return pl.pallas_call(
         residual_kernel,
         grid=(2048 // n,),
@@ -582,10 +588,7 @@
 
 
 def per_device(frames, targets, projection, phases, block_order):
-    me = lax.axis_index("wide") * 4 + lax.axis_index("narrow")
-    mask = (block_order[:STEPS] == me).astype(F32)
-    mask = jnp.broadcast_to(mask[:, None, None], (STEPS, 8, FEATS))
-    solved, fh, fl = fit(mask, projection[0], phases, frames.T, targets)
+    solved, fh, fl = fit(block_order, phases, projection[0], frames.T, targets)
     return residual_of(targets, solved.reshape(2048, 1024), fh, fl)
 
 

time: 184 us -> 183 us (level)
  no operation moved by 1% of the time
where the time goes in v5:
time: 183 us
  Pallas kernels  182 us (99%)
    pallas_call x1, Pallas kernels, fit(): pl.pallas_call(fit_kernel, out_shape=(jax.ShapeDtypeStruct((2, 4, 4, 4, 1...  162 us
    pallas_call x1, Pallas kernels, residual_of(): pl.pallas_call(residual_kernel, grid=(2048 // n,), out_shape=(jax.ShapeDt...  20 us

profile of v5, /device:TPU:1, one launch (start us, length us, event | category | flops | bytes accessed | tf_op | source)
XLA Modules:
  0.0 182.8 jit_solution(10352160505324306563)
XLA Ops:
  0.6 162.1 %shard_map.68 = (f32[2,4,4,4,16,1024]{5,4,3,2,1,0:T(8,128)}, bf16[1024,1024]{1,0:T(8,128)(2,1)}, bf16[1024,1024]{1,0:T(8,128)(2,1)}) custom-call(s32[128]{0:T(128)} %visited.1, f32[1,512]{1,0:T(1,128)} %phases.1, f32[440,512]{1,0:T(8,128)} %bitcast.5, f32[440,1024]{1,0:T(8,128)} %bitcast.4, f32[1024,2048]{1,0:T(8,128)} %targets.1), custom_call_target="tpu_custom_call" | custom-call | tf_op jit(solution)/shard_map/pallas_call | solution.py:508
  162.7 20.0 %shard_map.69 = (f32[1024,2048]{1,0:T(8,128)}, f32[2,512,2048]{2,1,0:T(8,128)}) custom-call(f32[1024,2048]{1,0:T(8,128)} %targets.1, f32[2048,1024]{1,0:T(8,128)} %bitcast.3, bf16[1024,1024]{1,0:T(8,128)(2,1)} %get-tuple-element.6.fh, bf16[1024,1024]{1,0:T(8,128)(2,1)} %get-tuple-element.7.fl), custom_call_target="tpu_custom_call" | custom-call | tf_op jit(solution)/shard_map/pallas_call | solution.py:569

commit v6 on v5

--- a/solution.py
+++ b/solution.py
@@ -185,14 +185,15 @@
 
 
 def inverse128(a, beside):
-    def quarter(q, a):
-        beside(q)
+    def half(h, a):
+        beside(2 * h)
+        beside(2 * h + 1)
         tiles = [a[8 * t : 8 * t + 8] for t in range(16)]
-        for k in range(4):
+        for k in range(8):
             tiles = eight_pivots(tiles, 8 * k)
-        return pltpu.roll(jnp.concatenate(tiles[4:] + tiles[:4], axis=0), 96, 1)
-
-    return lax.fori_loop(0, 4, quarter, a)
+        return pltpu.roll(jnp.concatenate(tiles[8:] + tiles[:8], axis=0), 64, 1)
+
+    return lax.fori_loop(0, 2, half, a)
 
 
 def block_at(k):

time: 183 us -> 183 us (level)
  no operation moved by 1% of the time
where the time goes in v6:
time: 183 us
  Pallas kernels  182 us (99%)
    pallas_call x1, Pallas kernels, fit(): pl.pallas_call(fit_kernel, out_shape=(jax.ShapeDtypeStruct((2, 4, 4, 4, 1...  162 us
    pallas_call x1, Pallas kernels, residual_of(): pl.pallas_call(residual_kernel, grid=(2048 // n,), out_shape=(jax.ShapeDt...  20 us

profile of v6, /device:TPU:1, one launch (start us, length us, event | category | flops | bytes accessed | tf_op | source)
XLA Modules:
  0.0 182.6 jit_solution(11690639982724539484)
XLA Ops:
  0.6 161.9 %shard_map.68 = (f32[2,4,4,4,16,1024]{5,4,3,2,1,0:T(8,128)}, bf16[1024,1024]{1,0:T(8,128)(2,1)}, bf16[1024,1024]{1,0:T(8,128)(2,1)}) custom-call(s32[128]{0:T(128)} %visited.1, f32[1,512]{1,0:T(1,128)} %phases.1, f32[440,512]{1,0:T(8,128)} %bitcast.5, f32[440,1024]{1,0:T(8,128)} %bitcast.4, f32[1024,2048]{1,0:T(8,128)} %targets.1), custom_call_target="tpu_custom_call" | custom-call | tf_op jit(solution)/shard_map/pallas_call | solution.py:509
  162.6 20.0 %shard_map.69 = (f32[1024,2048]{1,0:T(8,128)}, f32[2,512,2048]{2,1,0:T(8,128)}) custom-call(f32[1024,2048]{1,0:T(8,128)} %targets.1, f32[2048,1024]{1,0:T(8,128)} %bitcast.3, bf16[1024,1024]{1,0:T(8,128)(2,1)} %get-tuple-element.6.fh, bf16[1024,1024]{1,0:T(8,128)(2,1)} %get-tuple-element.7.fl), custom_call_target="tpu_custom_call" | custom-call | tf_op jit(solution)/shard_map/pallas_call | solution.py:570
